TPU v7x, 32 devices: a whole 2x2x4 slice. The times are simulated.
32 devices in a mesh: walk: 8 (over z, x), vec: 4 (over y, core).
Axes of the slice: x: 2, y: 2, z: 4, core: 2. Of those that a mesh axis runs over, the one named last changes fastest.
Arguments:
- walkers: bfloat16 [16, 2432, 768], P('walk')
- chol: bfloat16 [4, 8, 384, 4096], P('vec', 'walk'), may hold values from -6 to 6
- owners: int32 [4, 2], P('vec'), may hold values from 0 to 7
- branch_src: int32 [16], P('walk'), may hold values from 0 to 15, as said below
Outputs:
- branched: bfloat16 [16, 2432, 768], P('walk')
- force_bias: float32 [16, 8, 2], P('walk', 'vec')
- exchange: float32 [16, 2], P('walk')
Inputs may be any that keep to these rules, and one draw needn't show every extreme that they name: `branch_src`: slot s takes its walker from the 2 walkers of block s // 2, or of the block before or after it (blocks taken cyclically).
All inputs are finite; a program needn't handle non-finite values.
Results may differ from a plain program's by a relative error of at most 0.0052.
Values may be sent and summed in bfloat16 or wider, within the bound.
A program may use at most 192 MiB of HBM per device.

v0:
```python
import jax
import jax.numpy as jnp
from jax import lax
from jax.sharding import PartitionSpec as P


def padded_2(shard, sides, width):
    for axis, dim in sides:
        size, length = (lax.axis_size(axis), shard.shape[dim])
        up = [(i, (i + 1) % size) for i in range(size)]
        down = [(j, i) for i, j in up]
        last = lax.slice_in_dim(shard, length - width, length, axis=dim)
        leading = lax.slice_in_dim(shard, 0, width, axis=dim)
        before = lax.ppermute(last, axis, up)
        after = lax.ppermute(leading, axis, down)
        shard = jnp.concatenate([before, shard, after], axis=dim)
    return shard


def from_root(block, axis, source):
    block = jnp.where(lax.axis_index(axis) == source, block, jnp.zeros_like(block))
    return lax.psum(block, axis)


def complex_block(part):
    half = part.shape[1] // 2
    lower = jnp.concatenate([-part[:, half:], part[:, :half]], axis=1)
    return jnp.concatenate([part, lower], axis=0)


def walker_terms(state, vectors):
    electrons = state.shape[1] // 2
    orbitals = state.shape[0] - electrons
    pbig = complex_block(state[:orbitals])
    obig = complex_block(state[orbitals:])
    biases = []
    ex_real = jnp.float32(0.0)
    ex_imag = jnp.float32(0.0)
    for matrix in vectors:
        mixed = jnp.dot(matrix, pbig, preferred_element_type=jnp.float32).astype(jnp.bfloat16)
        green = jnp.dot(mixed, obig, preferred_element_type=jnp.float32)
        real = green[:, :electrons]
        imag = green[:, electrons:]
        biases.append(jnp.stack([jnp.trace(real), jnp.trace(imag)]))
        ex_real = ex_real + jnp.sum(real * real.T - imag * imag.T)
        ex_imag = ex_imag + 2.0 * jnp.sum(real * imag.T)
    return (jnp.stack(biases), jnp.stack([ex_real, ex_imag]))


def all_terms(states, vectors):
    bias_rows = []
    energy_rows = []
    for slot in range(states.shape[0]):
        bias, energy = walker_terms(states[slot], vectors)
        bias_rows.append(bias)
        energy_rows.append(energy)
    partial_value = jnp.stack(energy_rows)
    total = lax.psum(partial_value, "vec")
    return (jnp.stack(bias_rows), -0.5 * total)


def neighbour_copies(walkers, relative, per_dev):
    padded = padded_2(walkers, (("walk", 0),), per_dev)
    return jnp.take(padded, relative, axis=0)


def shards(walkers, chol, owners, branch_src):
    per_dev = walkers.shape[0]
    own_matrix = chol[0, 0]
    roots = owners[0]
    vectors = []
    for index in range(roots.shape[0]):
        vectors.append(from_root(own_matrix, "walk", roots[index]))
    device = lax.axis_index("walk")
    total_slots = per_dev * lax.axis_size("walk")
    relative = (branch_src - (device - 1) * per_dev + total_slots) % total_slots
    branched = neighbour_copies(walkers, relative, per_dev)
    force_bias, exchange = all_terms(branched, vectors)
    return (branched, force_bias, exchange)


def solution(mesh):
    return jax.shard_map(
        shards,
        mesh=mesh,
        in_specs=(P("walk", None, None), P("vec", "walk", None, None), P("vec", None), P("walk")),
        out_specs=(P("walk", None, None), P("walk", "vec", None), P("walk", None)),
        check_vma=False,
    )
```

profile of v0, /device:TPU:0, one launch (start us, length us, event | category | flops | bytes accessed | tf_op | source)
XLA Modules:
  0.0 547.5 jit_solution(8044180042097920071)
XLA Ops:
  7.2 3.0 collective-permute-start
  10.2 3.1 collective-permute-start.1
  15.9 4.9 select_bitcast_fusion.1
  21.9 376.2 %collective-permute-done = bf16[2,2432,768]{2,1,0:T(8,128)(2,1)} collective-permute-done((bf16[2,2432,768]{2,1,0:T(8,128)(2,1)}, bf16[2,2432,768]{2,1,0:T(8,128)(2,1)}, u32[]{:S(2)}, u32[]{:S(2)}) %collective-permute-start) | collective-permute-done | bytes 7471136 | tf_op jit(solution)/shard_map/ppermute | solution.py:14
  398.1 6.6 %constant_dynamic-update-slice_fusion.2 = bf16[6,2432,768]{2,1,0:T(8,128)(2,1)} fusion(bf16[2,2432,768]{2,1,0:T(8,128)(2,1)} %collective-permute-done), kind=kLoop, calls=%fused_computation.61 | loop fusion | bytes 14942208
  404.7 3.5 constant_dynamic-update-slice_fusion.1
  408.2 6.6 %constant_dynamic-update-slice_fusion = bf16[6,2432,768]{2,1,0:T(8,128)(2,1)} fusion(bf16[6,2432,768]{2,1,0:T(8,128)(2,1)} %constant_dynamic-update-slice_fusion.1, bf16[2,2432,768]{2,1,0:T(8,128)(2,1)} %collective-permute-done.1), kind=kLoop, calls=%fused_computation.59 | loop fusion | bytes 14942208 | tf_op jit(solution)/shard_map/concatenate | solution.py:16
  414.8 9.9 %mini-gather-slice.3 = bf16[6,1152,768]{2,1,0:T(8,128)(2,1)} slice(bf16[6,2432,768]{2,1,0:T(8,128)(2,1)} %constant_dynamic-update-slice_fusion), slice={[0:6], [1280:2432], [0:768]} | slice | bytes 21233664 | tf_op jit(solution)/shard_map/jit(_take)/gather | solution.py:64
  424.7 10.0 %mini-gather-slice.2 = bf16[6,1280,768]{2,1,0:T(8,128)(2,1)} slice(bf16[6,2432,768]{2,1,0:T(8,128)(2,1)} %constant_dynamic-update-slice_fusion), slice={[0:6], [0:1280], [0:768]} | slice | bytes 23592960 | tf_op jit(solution)/shard_map/jit(_take)/gather | solution.py:64
  434.7 4.8 gather_fusion.1
  439.5 7.0 %gather_fusion = bf16[2,1280,768]{2,1,0:T(8,128)(2,1)} fusion(bf16[6,1280,768]{2,1,0:T(8,128)(2,1)} %mini-gather-slice.2, s32[1024]{0:T(1024)S(1)} %pad_clamp_fusion), kind=kCustom, calls=%fused_computation | custom fusion | bytes 7864328 | tf_op jit(solution)/shard_map/jit(_take)/gather | solution.py:64
  446.5 6.9 %maximum_select_fusion = bf16[2,2432,768]{2,1,0:T(8,128)(2,1)} fusion(bf16[2,1152,768]{2,1,0:T(8,128)(2,1)S(1)} %gather_fusion.1, bf16[2,1280,768]{2,1,0:T(8,128)(2,1)} %gather_fusion, pred[2]{0:T(512)(128)(4,1)S(1)} %get-tuple-element.21), kind=kLoop, calls=%fused_computation.2 | loop fusion | flops 18677760 | bytes 14942210 | tf_op jit(solution)/shard_map/jit(_take)/select_n | solution.py:64
  453.4 1.3 slice_bitcast_fusion.3
  456.8 3.2 slice_bitcast_fusion.1
  460.1 1.7 copy-done
  461.8 2.9 slice_negate_fusion
  464.6 8.8 %fusion.8 = f32[384,768]{1,0:T(8,128)} fusion(bf16[384,4096]{1,0:T(8,128)(2,1)} %get-tuple-element.19, bf16[2048,384]{1,0:T(8,128)(2,1)} %get-tuple-element.30, bf16[2048,384]{1,0:T(8,128)(2,1)} %get-tuple-element.29, bf16[2048,768]{1,0:T(8,128)(2,1)} %copy-done, bf16[384,384]{1,0:T(8,128)(2,1)} %get-tuple-element.43, ...), kind=kOutput, calls=%fused_computation.21 | convolution fusion | flops 2891612160 | bytes 11796480 | tf_op jit(solution)/shard_map/dot_general | solution.py:41
  473.4 8.8 %fusion.9 = f32[384,768]{1,0:T(8,128)} fusion(bf16[384,4096]{1,0:T(8,128)(2,1)} %get-tuple-element.20, bf16[2048,384]{1,0:T(8,128)(2,1)} %get-tuple-element.30, bf16[2048,384]{1,0:T(8,128)(2,1)} %get-tuple-element.29, bf16[2048,768]{1,0:T(8,128)(2,1)} %copy-done, bf16[384,384]{1,0:T(8,128)(2,1)} %get-tuple-element.43, ...), kind=kOutput, calls=%fused_computation.22 | convolution fusion | flops 2891612160 | bytes 11796480 | tf_op jit(solution)/shard_map/dot_general | solution.py:41
  482.2 7.8 %fusion.11 = f32[384,768]{1,0:T(8,128)} fusion(bf16[384,4096]{1,0:T(8,128)(2,1)} %get-tuple-element.20, bf16[2048,384]{1,0:T(8,128)(2,1)} %get-tuple-element.52, bf16[2048,384]{1,0:T(8,128)(2,1)} %get-tuple-element.53, bf16[2048,768]{1,0:T(8,128)(2,1)S(1)} %get-tuple-element.25, bf16[384,384]{1,0:T(8,128)(2,1)S(1)} %get-tuple-element.54, ...), kind=kOutput, calls=%fused_computation.24 | convolution fusion | flops 2891612160 | bytes 11796480 | tf_op jit(solution)/shard_map/dot_general | solution.py:41
  490.1 8.1 %fusion.10 = f32[384,768]{1,0:T(8,128)} fusion(bf16[384,4096]{1,0:T(8,128)(2,1)} %get-tuple-element.19, bf16[2048,384]{1,0:T(8,128)(2,1)} %get-tuple-element.52, bf16[2048,384]{1,0:T(8,128)(2,1)} %get-tuple-element.53, bf16[2048,768]{1,0:T(8,128)(2,1)S(1)} %get-tuple-element.25, bf16[384,384]{1,0:T(8,128)(2,1)S(1)} %get-tuple-element.54, ...), kind=kOutput, calls=%fused_computation.23 | convolution fusion | flops 2891612160 | bytes 11796480 | tf_op jit(solution)/shard_map/dot_general | solution.py:41
  498.2 2.2 slice_bitcast_fusion.6
  501.7 2.1 fusion.14
  505.7 2.1 copy.49
  509.0 2.1 copy.48
  512.2 2.1 copy.42
  514.3 2.2 copy.40
  516.6 2.2 fusion.16
  518.8 2.1 fusion.18
  521.7 1.6 multiply_reduce_fusion.2
  528.5 5.8 %psum.23 = f32[2,2]{1,0:T(2,128)S(1)} all-reduce(f32[2,2]{1,0:T(2,128)S(1)} %pad_maximum_fusion.1), channel_id=1, replica_groups=mesh['walk'=8,'vec'=4] {'vec'}, use_global_device_ids=true, to_apply=%region_18.19 | all-reduce | flops 4 | bytes 32 | tf_op jit(solution)/shard_map/psum | solution.py:58
  534.8 1.4 maximum_bitcast_fusion.5
  538.7 1.4 maximum_bitcast_fusion.2
  (64 shorter events, 14.6 us)
Async XLA Ops:
  7.2 457.5 %all-reduce.3.cloned.1.call-start = ((), (), s32[]{:S(2)}) async-start(), calls=%async_computation | async-start | bytes 12582912 | tf_op jit(solution)/shard_map/psum | solution.py:22
  7.2 390.9 %collective-permute-start = (bf16[2,2432,768]{2,1,0:T(8,128)(2,1)}, bf16[2,2432,768]{2,1,0:T(8,128)(2,1)}, u32[]{:S(2)}, u32[]{:S(2)}) collective-permute-start(bf16[2,2432,768]{2,1,0:T(8,128)(2,1)} %param.4), channel_id=1, source_target_pairs={{0,4},{4,8},{8,12},{12,16},{16,20},{20,24},{24,28},{28,0},{1,5},{5... | collective-permute-start | bytes 22413320 | tf_op jit(solution)/shard_map/ppermute | solution.py:14
  10.2 398.0 %collective-permute-start.1 = (bf16[2,2432,768]{2,1,0:T(8,128)(2,1)}, bf16[2,2432,768]{2,1,0:T(8,128)(2,1)}, u32[]{:S(2)}, u32[]{:S(2)}) collective-permute-start(bf16[2,2432,768]{2,1,0:T(8,128)(2,1)} %param.4), channel_id=1, source_target_pairs={{4,0},{8,4},{12,8},{16,12},{20,16},{24,20},{28,24},{0,28},{5,1},{9... | collective-permute-start | bytes 22413320 | tf_op jit(solution)/shard_map/ppermute | solution.py:15
  20.8 1.0 copy-start.15
  20.9 383.8 %slice-start = ((s8[7471104]{0:T(1024)(128)(4,1)}), s8[3276800]{0:T(1024)(128)(4,1)S(1)}, s32[]{:S(2)}) async-start(s8[7471104]{0:T(1024)(128)(4,1)} %bitcast.90), calls=%async_computation.1 | async-start | bytes 6553600
  21.9 382.8 %slice-start.1 = ((s8[7471104]{0:T(1024)(128)(4,1)}), s8[4194304]{0:T(1024)(128)(4,1)S(1)}, s32[]{:S(2)}) async-start(s8[7471104]{0:T(1024)(128)(4,1)} %bitcast.90), calls=%async_computation.2 | async-start | bytes 8388608
  454.8 0.8 copy-start.12
  454.8 1.0 copy-start.13
  460.1 1.7 copy-start
  498.2 3.3 slice-start.2
  500.4 4.4 copy-start.1
  501.7 6.2 %copy-start.4 = (f32[384,384]{0,1:T(8,128)}, f32[384,384]{0,1:T(8,128)S(1)}, u32[]{:S(2)}) copy-start(f32[384,384]{0,1:T(8,128)S(1)} %copy.50) | copy-start | bytes 1769476
  501.7 6.2 %copy-start.3 = (f32[384,768]{1,0:T(8,128)S(1)}, f32[384,768]{1,0:T(8,128)}, u32[]{:S(2)}) copy-start(f32[384,768]{1,0:T(8,128)} %fusion.10) | copy-start | bytes 3538948
  514.3 6.6 %copy-start.2 = (f32[384,768]{1,0:T(8,128)S(1)}, f32[384,768]{1,0:T(8,128)}, u32[]{:S(2)}) copy-start(f32[384,768]{1,0:T(8,128)} %fusion.11) | copy-start | bytes 3538948
  516.5 4.3 copy-start.6
  516.5 4.3 copy-start.11
  516.5 5.2 copy-start.5
  516.5 5.2 copy-start.7
  516.5 5.2 copy-start.8
  516.5 5.2 copy-start.9
  516.5 5.2 copy-start.10
  516.6 5.2 copy-start.14
Sparse Core Ops, SparseCore 0:
  21.0 389.7 all-reduce.2
where the time goes:
time: 548 us
  waiting for transfers between devices  376 us (69%)
  local copies, waits for them, and re-layouts  74.2 us (14%)
  matrix products  33.6 us (6%)
  other arithmetic  31.2 us (6%)
  between operations  20.5 us (4%)
  starting transfers between devices  6.16 us (1%)
  blocking collectives  5.78 us (1%)
    ppermute x1, waiting for transfers between devices, padded_2(): before = lax.ppermute(last, axis, up)  376 us
    dot_general x4, matrix products, walker_terms(): green = jnp.dot(mixed, obig, preferred_element_type=jnp.float32)  33.6 us
    gather x4, local copies, waits for them, and re-layouts, neighbour_copies(): return jnp.take(padded, relative, axis=0)  31.7 us
    unnamed x42, local copies, waits for them, and re-layouts  18.4 us
  transfers between devices with their start and end apart: 3, of which 1 were waited for; matrix products, arithmetic and copies ran while one was open for 13% of the time, Pallas kernels for 0%

commit v1 on v0

v1 whole, which is shorter than its diff:
```python
import functools

import jax
import jax.numpy as jnp
from jax import lax
from jax.experimental import pallas as pl
from jax.experimental.pallas import tpu as pltpu
from jax.sharding import PartitionSpec as P

MESH = pl.DeviceIdType.MESH
CHUNKS = 24


def flip(index):
    return index + 1 - 2 * lax.rem(index, 2)


def move_kernel(
    n_walk, n_vec, flags, slots, chol, walkers, out, partner, branched,
    home, away, own, up, down, cand, sel,
    bcast_send, home_sem, away_send, away_sem, relay_send,
    up_send, up_sem, down_send, down_sem,
    x_send, x_sem, d_send, d_sem, z_send, z_sem, local_sem, g_send, g_sem, self_sem,
):
    walk, vec = lax.axis_index("walk"), lax.axis_index("vec")
    rows = n_walk // 2
    row, col = walk // 2, lax.rem(walk, 2)
    low, high = lax.rem(vec, 2), vec // 2
    highs = n_vec // 2
    hub = low == col
    chunks, depth = home.shape[0], home.shape[1]
    piece = sel.shape[1]
    per_dev = walkers.shape[0]
    flip_walk, flip_vec = flip(walk), flip(vec)
    z_next = lax.rem(row + 1 - 2 * col + rows, rows)
    z_prev = lax.rem(row - 1 + 2 * col + rows, rows)
    z_to = {"walk": z_next * 2 + col, "vec": vec}
    z_from = {"walk": z_prev * 2 + col, "vec": vec}
    across = {"walk": flip_walk, "vec": vec}
    mate = {"walk": walk, "vec": flip_vec}
    above = {"walk": walk + 2, "vec": vec}
    below = {"walk": walk - 2, "vec": vec}

    def peer(j):
        return {"walk": walk, "vec": lax.rem(vec + j, n_vec)}

    bar = pltpu.get_barrier_semaphore()

    def hello(target):
        pl.semaphore_signal(bar, inc=1, device_id=target, device_id_type=MESH)

    hello(across)
    hello(z_to)
    hello(z_from)
    for j in range(1, n_vec):
        hello(peer(j))
    pl.semaphore_wait(bar, 3 + n_vec - 1)

    def remote(src, dst, send, recv, target):
        return pltpu.make_async_remote_copy(
            src_ref=src, dst_ref=dst, send_sem=send, recv_sem=recv,
            device_id=target, device_id_type=MESH)

    def chol_rows(k):
        return chol.at[0, 0, pl.ds(pl.multiple_of(k * depth, depth), depth)]

    def own_to_home(k):
        return pltpu.make_async_copy(chol_rows(k), home.at[k], home_sem.at[k])

    def own_to_mate(k):
        return remote(chol_rows(k), home.at[k], bcast_send.at[k], home_sem.at[k], mate)

    def own_across(k):
        return remote(chol_rows(k), away.at[k], away_send.at[k], away_sem.at[k], across)

    def away_to_mate(k):
        return remote(away.at[k], away.at[k], relay_send.at[k], away_sem.at[k], mate)

    def send_up(k):
        return remote(up.at[k], up.at[k], up_send.at[k], up_sem.at[k], above)

    def send_down(k):
        return remote(down.at[k], down.at[k], down_send.at[k], down_sem.at[k], below)

    def part(half, sub):
        return pl.ds(pl.multiple_of((half * highs + sub) * piece, piece), piece)

    def sub_of(j):
        return lax.rem(high + j, highs)

    def walker_across(w, j):
        at = part(low, sub_of(j))
        return remote(walkers.at[w, at], partner.at[w, at], x_send.at[w, j], x_sem.at[w, j], across)

    def walker_mate(w, j):
        at = part(low, sub_of(j))
        return remote(partner.at[w, at], partner.at[w, at], d_send.at[w, j], d_sem.at[w, j], mate)

    far_base = col * 2 * per_dev
    near_base = (1 - col) * 2 * per_dev
    mine = part(low, high)

    def walker_z(w):
        return remote(partner.at[w, mine], cand.at[far_base + w], z_send.at[w], z_sem.at[w], z_to)

    def own_cand(w):
        return pltpu.make_async_copy(walkers.at[w, mine], cand.at[per_dev + w], local_sem.at[w])

    def near_cand(w):
        return pltpu.make_async_copy(partner.at[w, mine], cand.at[near_base + w], local_sem.at[per_dev + w])

    def gather(s, j):
        return remote(sel.at[s], branched.at[s, mine], g_send.at[s, j - 1], g_sem.at[s, j - 1], peer(j))

    def gather_self(s):
        return pltpu.make_async_copy(sel.at[s], branched.at[s, mine], self_sem.at[s])

    def each(lo, hi, f):
        def body(k, carry):
            f(k)
            return carry
        lax.fori_loop(lo, hi, body, 0)

    @pl.when(hub)
    def _():
        def start(k):
            own_to_home(k).start()
            own_to_mate(k).start()
        for w in range(per_dev):
            walker_across(w, 0).start()
        each(0, chunks, start)

    @pl.when(jnp.logical_not(hub))
    def _():
        cut = [chunks * (w + 1) // (per_dev + 1) for w in range(per_dev)]
        at = 0
        for w in range(per_dev):
            each(at, cut[w], lambda k: own_across(k).start())
            walker_across(w, 0).start()
            at = cut[w]
        each(at, chunks, lambda k: own_across(k).start())

    for j in range(1, highs):
        for w in range(per_dev):
            walker_across(w, j).start()
    for w in range(per_dev):
        own_cand(w).start()

    last = rows - 1
    here = flags[0] == 1
    below_or_here = flags[1] == 1
    from_home = flags[2] == 1

    def step(i):
        @pl.when(i < chunks)
        def _():
            @pl.when(hub)
            def _():
                own_across(i).wait_recv()
                away_to_mate(i).start()
                own_to_home(i).wait()

            @pl.when(jnp.logical_not(hub))
            def _():
                own_to_mate(i).wait_recv()
                away_to_mate(i).wait_recv()

            own[i] = jnp.where(from_home, home[i], away[i])

        ku = i - row
        kd = i - (last - row)

        @pl.when(jnp.logical_and(ku >= 0, ku < chunks))
        def _():
            @pl.when(row == 0)
            def _():
                up[ku] = own[ku]

            @pl.when(row > 0)
            def _():
                send_up(ku).wait_recv()
                up[ku] = jnp.where(here, own[ku], up[ku])

            @pl.when(row < last)
            def _():
                send_up(ku).start()

        @pl.when(jnp.logical_and(kd >= 0, kd < chunks))
        def _():
            @pl.when(row == last)
            def _():
                down[kd] = own[kd]

            @pl.when(row < last)
            def _():
                send_down(kd).wait_recv()
                down[kd] = jnp.where(here, own[kd], down[kd])

            @pl.when(row > 0)
            def _():
                send_down(kd).start()

    def arrive(w):
        walker_across(w, 0).wait_recv()
        walker_z(w).start()
        walker_mate(w, 0).start()
        near_cand(w).start()

    total = chunks + last
    at = 0
    for w in range(per_dev):
        cut = chunks * (w + 1) // (per_dev + 1) + 2
        each(at, cut, step)
        arrive(w)
        at = cut
    each(at, total, step)

    for j in range(1, highs):
        for w in range(per_dev):
            walker_across(w, j).wait_recv()
            walker_mate(w, j).start()

    def finish(k):
        out[pl.ds(pl.multiple_of(k * depth, depth), depth), :] = jnp.where(below_or_here, up[k], down[k])

    each(0, chunks, finish)

    for w in range(per_dev):
        own_cand(w).wait()
        near_cand(w).wait()
        walker_z(w).wait_recv()
    lines = 16
    for s in range(per_dev):
        index = slots[s]

        def pick(t, s=s, index=index):
            at = pl.ds(pl.multiple_of(t * lines, lines), lines)
            sel[s, at, :] = cand[index, at, :]

        each(0, piece // lines, pick)
        for j in range(1, n_vec):
            gather(s, j).start()
        gather_self(s).start()

    @pl.when(hub)
    def _():
        def ended(k):
            own_to_mate(k).wait_send()
            away_to_mate(k).wait_send()
        each(0, chunks, ended)

    @pl.when(jnp.logical_not(hub))
    def _():
        each(0, chunks, lambda k: own_across(k).wait_send())

    @pl.when(row < last)
    def _():
        each(0, chunks, lambda k: send_up(k).wait_send())

    @pl.when(row > 0)
    def _():
        each(0, chunks, lambda k: send_down(k).wait_send())

    for w in range(per_dev):
        for j in range(highs):
            walker_across(w, j).wait_send()
            walker_mate(w, j).wait()
        walker_z(w).wait_send()
    for s in range(per_dev):
        for j in range(1, n_vec):
            gather(s, j).wait()
        gather_self(s).wait()


def move(n_walk, n_vec, flags, slots, chol, walkers):
    per_dev, height, width = walkers.shape
    electrons, orbitals = chol.shape[2:]
    chunks = CHUNKS if electrons % (CHUNKS * 16) == 0 else 1
    depth = electrons // chunks
    highs = n_vec // 2
    big = pltpu.VMEM((chunks, depth, orbitals), chol.dtype)
    dma = pltpu.SemaphoreType.DMA
    any_spec = pl.BlockSpec(memory_space=pl.ANY)
    smem = pl.BlockSpec(memory_space=pltpu.SMEM)
    same = jax.ShapeDtypeStruct(walkers.shape, walkers.dtype)
    return pl.pallas_call(
        functools.partial(move_kernel, n_walk, n_vec),
        out_shape=(jax.ShapeDtypeStruct((electrons, orbitals), chol.dtype), same, same),
        in_specs=[smem, smem, any_spec, any_spec],
        out_specs=(pl.BlockSpec(memory_space=pltpu.VMEM), any_spec, any_spec),
        scratch_shapes=[
            big, big, big, big, big,
            pltpu.VMEM((3 * per_dev, height // n_vec, width), walkers.dtype),
            pltpu.VMEM((per_dev, height // n_vec, width), walkers.dtype),
        ] + [dma((chunks,))] * 9 + [
            dma((per_dev, highs)), dma((per_dev, highs)),
            dma((per_dev, highs)), dma((per_dev, highs)),
            dma((per_dev,)), dma((per_dev,)), dma((2 * per_dev,)),
            dma((per_dev, n_vec - 1)), dma((per_dev, n_vec - 1)), dma((per_dev,)),
        ],
        compiler_params=pltpu.CompilerParams(
            collective_id=0, has_side_effects=True, vmem_limit_bytes=48 * 1024 * 1024),
        name="move",
    )(flags, slots, chol, walkers)


def terms_kernel(per_dev, matrix, near, far, out):
    electrons = matrix.shape[0]
    orbitals = matrix.shape[1] // 2
    ahead = pl.program_id(0) < per_dev

    def work(state):
        a_re, a_im = matrix[:, :orbitals], matrix[:, orbitals:]
        p = state[0, :orbitals, :]
        o = state[0, orbitals:, :]
        x = jnp.dot(a_re, p, preferred_element_type=jnp.float32)
        y = jnp.dot(a_im, p, preferred_element_type=jnp.float32)
        m_re = (x[:, :electrons] - y[:, electrons:]).astype(jnp.bfloat16)
        m_im = (x[:, electrons:] + y[:, :electrons]).astype(jnp.bfloat16)
        u = jnp.dot(m_re, o, preferred_element_type=jnp.float32)
        v = jnp.dot(m_im, o, preferred_element_type=jnp.float32)
        g_re = u[:, :electrons] - v[:, electrons:]
        g_im = u[:, electrons:] + v[:, :electrons]
        t_re, t_im = g_re.T, g_im.T
        eye = (lax.broadcasted_iota(jnp.int32, g_re.shape, 0)
               == lax.broadcasted_iota(jnp.int32, g_re.shape, 1))
        values = [
            jnp.sum(jnp.where(eye, g_re, 0.0)),
            jnp.sum(jnp.where(eye, g_im, 0.0)),
            jnp.sum(g_re * t_re - g_im * t_im),
            2.0 * jnp.sum(g_re * t_im),
        ]
        lane = lax.broadcasted_iota(jnp.int32, out.shape, 2)
        row = jnp.zeros(out.shape, jnp.float32)
        for n, value in enumerate(values):
            row = jnp.where(lane == n, value, row)
        out[...] = row

    @pl.when(ahead)
    def _():
        work(near)

    @pl.when(jnp.logical_not(ahead))
    def _():
        work(far)


def terms(matrix, near, far):
    per_dev, height, width = near.shape
    return pl.pallas_call(
        functools.partial(terms_kernel, per_dev),
        grid=(2 * per_dev,),
        out_shape=jax.ShapeDtypeStruct((2 * per_dev, 8, 128), jnp.float32),
        in_specs=[
            pl.BlockSpec(matrix.shape, lambda i: (0, 0)),
            pl.BlockSpec((1, height, width), lambda i: (jnp.minimum(i, per_dev - 1), 0, 0)),
            pl.BlockSpec((1, height, width), lambda i: (jnp.maximum(i - per_dev, 0), 0, 0)),
        ],
        out_specs=pl.BlockSpec((1, 8, 128), lambda i: (i, 0, 0)),
        compiler_params=pltpu.CompilerParams(vmem_limit_bytes=56 * 1024 * 1024),
        name="terms",
    )(matrix, near, far)[:, 0, :4]


def shards(n_walk, n_vec, walkers, chol, owners, branch_src):
    per_dev = walkers.shape[0]
    walk, vec = lax.axis_index("walk"), lax.axis_index("vec")
    row, col, low = walk // 2, walk % 2, vec % 2
    swap = [(i, i + 1 - 2 * (i % 2)) for i in range(n_vec)]
    mate_roots = lax.ppermute(owners[0], "vec", swap)
    roots = jnp.where(low == col, owners[0], mate_roots)
    root = jnp.take(roots, low)
    flags = jnp.stack([root // 2 == row, root // 2 <= row, root % 2 == col]).astype(jnp.int32)
    total = per_dev * n_walk
    relative = ((branch_src - (walk - 1) * per_dev + total) % total).astype(jnp.int32)
    matrix, partner, branched = move(n_walk, n_vec, flags, relative, chol, walkers)
    values = terms(matrix, walkers, partner)
    table = lax.all_gather(values, ("walk", "vec"))
    table = table.reshape(n_walk // 2, 2, n_vec // 2, 2, 2, per_dev, 4)
    even, odd = table[:, 0], table[:, 1]
    near_first = jnp.stack([even[:, :, :, 0], odd[:, :, :, 1]], axis=2)
    far_first = jnp.stack([even[:, :, :, 1], odd[:, :, :, 0]], axis=2)
    both = jnp.stack([near_first, far_first], axis=1)
    both = jnp.transpose(both, (0, 1, 5, 2, 3, 4, 6)).reshape(total, n_vec, 2, 4)
    chosen = jnp.take(both, branch_src, axis=0)
    bias = lax.dynamic_slice_in_dim(chosen, vec, 1, axis=1)[:, 0, :, :2]
    energy = -0.5 * jnp.sum(chosen[..., 2:], axis=(1, 2))
    return (branched, bias, energy)


def solution(mesh):
    n_walk, n_vec = mesh.shape["walk"], mesh.shape["vec"]
    return jax.shard_map(
        functools.partial(shards, n_walk, n_vec),
        mesh=mesh,
        in_specs=(P("walk", None, None), P("vec", "walk", None, None), P("vec", None), P("walk")),
        out_specs=(P("walk", None, None), P("walk", "vec", None), P("walk", None)),
        check_vma=False,
    )
```

time: 548 us -> 323 us (0.59)
  waiting for transfers between devices: 376 us -> 0.01 us
  Pallas kernels: 0 us -> 269 us
  local copies, waits for them, and re-layouts: 74.2 us -> 10.9 us
  matrix products: 33.6 us -> 0 us
  blocking collectives: 5.78 us -> 38.4 us
  other arithmetic: 31.2 us -> 2.88 us
  between operations: 20.5 us -> 1.42 us
  starting transfers between devices: 6.16 us -> 0.56 us
    ppermute x2 -> x1, waiting for transfers between devices: 376 us -> 0.01 us  [shards(): mate_roots = lax.ppermute(owners[0], 'vec', swap)]
    pallas_call x0 -> x2, Pallas kernels: none -> 269 us  [the longest x1 249 us: move(): pl.pallas_call(functools.partial(move_kernel, n_walk, n_vec), out_shape=(...]
    all_gather x0 -> x1, blocking collectives: none -> 38.4 us  [shards(): table = lax.all_gather(values, ('walk', 'vec'))]
    dot_general x4 -> x0, matrix products: 33.6 us -> none  [walker_terms(): green = jnp.dot(mixed, obig, preferred_element_type=jnp.float32)]
    gather x4 -> x1, local copies, waits for them, and re-layouts: 31.7 us -> 0.57 us  [shards(): chosen = jnp.take(both, branch_src, axis=0)]
    select_n x2 -> x3, other arithmetic: 11.8 us -> 1.4 us  [the longest x2 0.74 us: shards(): chosen = jnp.take(both, branch_src, axis=0)]
    unnamed x42 -> x3, local copies, waits for them, and re-layouts: 18.4 us -> 8.35 us
    transpose x6 -> x1, local copies, waits for them, and re-layouts: 9.62 us -> 0.02 us  [shards(): jnp.transpose(both, (0, 1, 5, 2, 3, 4, 6)).reshape(total, n_vec, 2, 4)]
  transfers between devices with their start and end apart: 3 -> 1, of which waited for: 1 -> 0; matrix products, arithmetic and copies ran while one was open for 13% -> 0% of each run, Pallas kernels for 0% -> 0%
where the time goes in v1:
time: 323 us
  Pallas kernels  269 us (83%)
  blocking collectives  38.4 us (12%)
  local copies, waits for them, and re-layouts  10.9 us (3%)
    pallas_call x1, Pallas kernels, move(): pl.pallas_call(functools.partial(move_kernel, n_walk, n_vec), out_shape=(...  249 us
    all_gather x1, blocking collectives, shards(): table = lax.all_gather(values, ('walk', 'vec'))  38.4 us
    pallas_call x1, Pallas kernels, terms(): pl.pallas_call(functools.partial(terms_kernel, per_dev), grid=(2 * per_de...  19.3 us
    unnamed x3, local copies, waits for them, and re-layouts  8.35 us
  transfers between devices with their start and end apart: 1, of which 0 were waited for; matrix products, arithmetic and copies ran while one was open for 0% of the time, Pallas kernels for 0%

profile of v1, /device:TPU:0, one launch (start us, length us, event | category | flops | bytes accessed | tf_op | source)
XLA Modules:
  0.0 322.7 jit_solution(6890453231398930469)
XLA Ops:
  0.6 0.6 collective-permute-start
  1.2 0.7 compare_and_fusion
  1.8 0.7 compare_select_fusion
  2.5 0.0 collective-permute-done
  2.5 0.7 broadcast_select_fusion.1
  3.2 0.6 dynamic-slice.2
  4.5 0.1 add_convert_fusion.flags
  4.6 249.2 %move.1 = (bf16[384,4096]{1,0:T(8,128)(2,1)S(1)}, bf16[2,2432,768]{2,1,0:T(8,128)(2,1)}, bf16[2,2432,768]{2,1,0:T(8,128)(2,1)}) custom-call(s32[3]{0:T(128)S(1)} %add_convert_fusion.flags, s32[2]{0:T(128)S(1)} %get-tuple-element.27.slots, bf16[1,1,384,4096]{3,2,1,0:T(8,128)(2,1)} %chol.1, bf16[2,2432,768]{2,1,0:T(8,128)(2,1)} %near.1), custom_call_target="tpu_custom_call" | custom-call | tf_op jit(solution)/shard_map/move/pallas_call | solution.py:286
  253.8 0.0 copy-start
  253.8 1.7 copy-done
  255.4 19.3 %terms.1 = f32[4,8,128]{2,1,0:T(8,128)} custom-call(bf16[384,4096]{1,0:T(8,128)(2,1)} %copy-done, bf16[2,2432,768]{2,1,0:T(8,128)(2,1)} %near.1, bf16[2,2432,768]{2,1,0:T(8,128)(2,1)} %get-tuple-element.8.far), custom_call_target="tpu_custom_call" | custom-call | tf_op jit(solution)/shard_map/terms/pallas_call | solution.py:350
  274.7 0.7 slice.43
  275.5 38.4 %all-gather = f32[128,1,4]{2,1,0:T(1,128)S(1)} all-gather(f32[4,1,4]{2,1,0:T(1,128)S(1)} %slice.43), channel_id=2, replica_groups=mesh['walk'=8,'vec'=4] {'walk','vec'}, dimensions={0}, use_global_device_ids=true | all-gather | bytes 2112 | tf_op jit(solution)/shard_map/all_gather | solution.py:378
  314.1 0.6 gather_fusion
  314.7 0.1 broadcast_select_fusion
  314.8 0.1 slice_reduce_fusion
  314.9 0.6 constant_dynamic-slice_fusion
  315.4 0.6 broadcast_multiply_fusion
  316.0 6.7 %copy.22 = bf16[2,2432,768]{2,1,0:T(8,128)(2,1)} copy(bf16[2,2432,768]{2,1,0:T(8,128)(2,1)} %get-tuple-element.33) | data formatting | bytes 14942208
  (10 shorter events, 0.2 us)
Async XLA Ops:
  0.6 1.9 collective-permute-start
  253.8 1.7 copy-start

commit v2 on v1

v2 whole, which is shorter than its diff:
```python
import functools

import jax
import jax.numpy as jnp
from jax import lax
from jax.experimental import pallas as pl
from jax.experimental.pallas import tpu as pltpu
from jax.sharding import PartitionSpec as P

MESH = pl.DeviceIdType.MESH
CHUNKS = 24
PARTS = 2
EARLY = (5, 9, 12, 15)


def flip(index):
    return index + 1 - 2 * lax.rem(index, 2)


def walker_values(matrix, state):
    electrons = matrix.shape[0]
    orbitals = matrix.shape[1] // 2
    p = state[:orbitals, :]
    o = state[orbitals:, :]
    x = jnp.dot(matrix[:, :orbitals], p, preferred_element_type=jnp.float32)
    y = jnp.dot(matrix[:, orbitals:], p, preferred_element_type=jnp.float32)
    m_re = (x[:, :electrons] - y[:, electrons:]).astype(jnp.bfloat16)
    m_im = (x[:, electrons:] + y[:, :electrons]).astype(jnp.bfloat16)
    u = jnp.dot(m_re, o, preferred_element_type=jnp.float32)
    v = jnp.dot(m_im, o, preferred_element_type=jnp.float32)
    g_re = u[:, :electrons] - v[:, electrons:]
    g_im = u[:, electrons:] + v[:, :electrons]
    t_re, t_im = g_re.T, g_im.T
    eye = (lax.broadcasted_iota(jnp.int32, g_re.shape, 0)
           == lax.broadcasted_iota(jnp.int32, g_re.shape, 1))
    return [
        jnp.sum(jnp.where(eye, g_re, 0.0)),
        jnp.sum(jnp.where(eye, g_im, 0.0)),
        jnp.sum(g_re * t_re - g_im * t_im),
        2.0 * jnp.sum(g_re * t_im),
    ]


def step_kernel(
    n_walk, n_vec, flags, slots, chol, walkers, table, partner, branched,
    home, away, own, up, down, cand_0, cand_1, sel, matrix, state, result,
    bcast_send, home_sem, away_send, away_sem, relay_send,
    up_send, up_sem, down_send, down_sem,
    x_send, x_sem, z_send, z_sem, local_sem,
    y_send, y_sem, d_send, d_sem, r_send, r_sem,
    by_send, by_sem, bd_send, bd_sem, br_send, br_sem, self_sem,
    load_sem, t_send, t_sem,
):
    walk, vec = lax.axis_index("walk"), lax.axis_index("vec")
    rows = n_walk // 2
    row, col = walk // 2, lax.rem(walk, 2)
    low = lax.rem(vec, 2)
    hub = low == col
    cand = (cand_0, cand_1)
    chunks, depth = home.shape[0], home.shape[1]
    per_dev = walkers.shape[0]
    quarter = sel.shape[1]
    piece = quarter // PARTS
    pieces = [(w, t) for t in range(PARTS) for w in range(per_dev)]
    flip_walk, flip_vec = flip(walk), flip(vec)
    far_vec = lax.rem(vec + 2, n_vec)
    z_next = lax.rem(row + 1 - 2 * col + rows, rows)
    z_to = {"walk": z_next * 2 + col, "vec": vec}
    across = {"walk": flip_walk, "vec": vec}
    mate = {"walk": walk, "vec": flip_vec}
    over = {"walk": walk, "vec": far_vec}
    above = {"walk": walk + 2, "vec": vec}
    below = {"walk": walk - 2, "vec": vec}
    row_up, row_down = lax.rem(row + 1, rows), lax.rem(row + rows - 1, rows)

    place = col * n_vec + vec
    readers = [({"walk": walk, "vec": lax.rem(vec + j, n_vec)}, place) for j in range(1, n_vec)]
    readers += [({"walk": flip_walk, "vec": lax.rem(vec + j, n_vec)}, place) for j in range(n_vec)]
    readers += [({"walk": row_up * 2, "vec": lax.rem(vec + j, n_vec)}, place + 2 * n_vec) for j in range(n_vec)]
    readers += [({"walk": row_down * 2 + 1, "vec": lax.rem(vec + j, n_vec)}, place + 2 * n_vec) for j in range(n_vec)]

    bar = pltpu.get_barrier_semaphore()
    for target in (
        [t for t, _ in readers[:2 * n_vec - 1]]
        + [{"walk": r * 2 + c, "vec": lax.rem(vec + j, n_vec)}
           for r in (row_up, row_down) for c in range(2) for j in range(n_vec)]
    ):
        pl.semaphore_signal(bar, inc=1, device_id=target, device_id_type=MESH)
    pl.semaphore_wait(bar, 6 * n_vec - 1)

    def remote(src, dst, send, recv, target):
        return pltpu.make_async_remote_copy(
            src_ref=src, dst_ref=dst, send_sem=send, recv_sem=recv,
            device_id=target, device_id_type=MESH)

    def chol_rows(k):
        return chol.at[0, 0, pl.ds(pl.multiple_of(k * depth, depth), depth)]

    def own_to_home(k):
        return pltpu.make_async_copy(chol_rows(k), home.at[k], home_sem.at[k])

    def own_to_mate(k):
        return remote(chol_rows(k), home.at[k], bcast_send.at[k], home_sem.at[k], mate)

    def own_across(k):
        return remote(chol_rows(k), away.at[k], away_send.at[k], away_sem.at[k], across)

    def away_to_mate(k):
        return remote(away.at[k], away.at[k], relay_send.at[k], away_sem.at[k], mate)

    def send_up(k):
        return remote(up.at[k], up.at[k], up_send.at[k], up_sem.at[k], above)

    def send_down(k):
        return remote(down.at[k], down.at[k], down_send.at[k], down_sem.at[k], below)

    def part(index, t):
        return pl.ds(pl.multiple_of(index * quarter + t * piece, piece), piece)

    def inner(t):
        return pl.ds(t * piece, piece)

    far_base = col * 2 * per_dev
    near_base = (1 - col) * 2 * per_dev

    def walker_across(w, t):
        at = part(vec, t)
        return remote(walkers.at[w, at], partner.at[w, at], x_send.at[w, t], x_sem.at[w, t], across)

    def walker_z(w, t):
        return remote(partner.at[w, part(vec, t)], cand[t].at[far_base + w],
                      z_send.at[w, t], z_sem.at[w, t], z_to)

    def own_cand(w, t):
        return pltpu.make_async_copy(
            walkers.at[w, part(vec, t)], cand[t].at[per_dev + w], local_sem.at[w, t])

    def near_cand(w, t):
        return pltpu.make_async_copy(
            partner.at[w, part(vec, t)], cand[t].at[near_base + w], local_sem.at[w, PARTS + t])

    def walker_y(w, t):
        at = part(vec, t)
        return remote(partner.at[w, at], partner.at[w, at], y_send.at[w, t], y_sem.at[w, t], over)

    def walker_mate(w, t):
        at = part(vec, t)
        return remote(partner.at[w, at], partner.at[w, at], d_send.at[w, t], d_sem.at[w, t], mate)

    def walker_relay(w, t):
        at = part(far_vec, t)
        return remote(partner.at[w, at], partner.at[w, at], r_send.at[w, t], r_sem.at[w, t], mate)

    def slot_y(s, t):
        return remote(sel.at[s, inner(t)], branched.at[s, part(vec, t)], by_send.at[s, t], by_sem.at[s, t], over)

    def slot_mate(s, t):
        return remote(sel.at[s, inner(t)], branched.at[s, part(vec, t)], bd_send.at[s, t], bd_sem.at[s, t], mate)

    def slot_relay(s, t):
        at = part(far_vec, t)
        return remote(branched.at[s, at], branched.at[s, at], br_send.at[s, t], br_sem.at[s, t], mate)

    def slot_self(s, t):
        return pltpu.make_async_copy(sel.at[s, inner(t)], branched.at[s, part(vec, t)], self_sem.at[s, t])

    def each(lo, hi, f):
        def body(k, carry):
            f(k)
            return carry
        lax.fori_loop(lo, hi, body, 0)

    for w, t in pieces:
        own_cand(w, t).start()

    @pl.when(hub)
    def _():
        def start(k):
            own_to_home(k).start()
            own_to_mate(k).start()
        for w, t in pieces:
            walker_across(w, t).start()
        each(0, chunks, start)

    @pl.when(jnp.logical_not(hub))
    def _():
        each(0, chunks, lambda k: own_across(k).start())
        for w, t in pieces:
            walker_across(w, t).start()

    for w in range(per_dev):
        pltpu.make_async_copy(walkers.at[w], state.at[w], load_sem.at[w]).start()

    last = rows - 1
    here = flags[0] == 1
    below_or_here = flags[1] == 1
    from_home = flags[2] == 1

    def step(i):
        @pl.when(i < chunks)
        def _():
            @pl.when(hub)
            def _():
                own_across(i).wait_recv()
                away_to_mate(i).start()
                own_to_home(i).wait()

            @pl.when(jnp.logical_not(hub))
            def _():
                own_to_mate(i).wait_recv()
                away_to_mate(i).wait_recv()

            own[i] = jnp.where(from_home, home[i], away[i])

        ku = i - row
        kd = i - (last - row)

        @pl.when(jnp.logical_and(ku >= 0, ku < chunks))
        def _():
            @pl.when(row == 0)
            def _():
                up[ku] = own[ku]

            @pl.when(row > 0)
            def _():
                send_up(ku).wait_recv()
                up[ku] = jnp.where(here, own[ku], up[ku])

            @pl.when(row < last)
            def _():
                send_up(ku).start()

        @pl.when(jnp.logical_and(kd >= 0, kd < chunks))
        def _():
            @pl.when(row == last)
            def _():
                down[kd] = own[kd]

            @pl.when(row < last)
            def _():
                send_down(kd).wait_recv()
                down[kd] = jnp.where(here, own[kd], down[kd])

            @pl.when(row > 0)
            def _():
                send_down(kd).start()

    def arrive(w, t):
        walker_across(w, t).wait_recv()
        walker_z(w, t).start()
        walker_y(w, t).start()
        walker_mate(w, t).start()
        near_cand(w, t).start()

    total = chunks + last
    at = 0
    for n, (w, t) in enumerate(pieces):
        cut = min(EARLY[min(n, len(EARLY) - 1)], total)
        each(at, cut, step)
        at = cut

        @pl.when(jnp.logical_not(hub))
        def _():
            arrive(w, t)
    each(at, total, step)

    @pl.when(hub)
    def _():
        for w, t in pieces:
            arrive(w, t)

    def finish(k):
        matrix[pl.ds(pl.multiple_of(k * depth, depth), depth), :] = jnp.where(below_or_here, up[k], down[k])

    each(0, chunks, finish)

    lines = 16

    def select(t):
        for w in range(per_dev):
            near_cand(w, t).wait()
            walker_z(w, t).wait_recv()
        for s in range(per_dev):
            index = slots[s]

            def pick(n, s=s, index=index):
                at = pl.ds(pl.multiple_of(t * piece + n * lines, lines), lines)
                sel[s, at, :] = cand[t][index, pl.ds(pl.multiple_of(n * lines, lines), lines), :]

            each(0, piece // lines, pick)
            slot_y(s, t).start()
            slot_mate(s, t).start()
            slot_self(s, t).start()

    for w, t in pieces:
        own_cand(w, t).wait()

    @pl.when(jnp.logical_not(hub))
    def _():
        for t in range(PARTS):
            select(t)

    for w, t in pieces:
        walker_y(w, t).wait_recv()
        walker_relay(w, t).start()
    for w, t in pieces:
        walker_mate(w, t).wait_recv()
        walker_relay(w, t).wait_recv()

    def load(i):
        return pltpu.make_async_copy(partner.at[i], state.at[i], load_sem.at[i])

    sub = lax.broadcasted_iota(jnp.int32, result.shape, 0)
    lane = lax.broadcasted_iota(jnp.int32, result.shape, 1)
    result[...] = jnp.zeros_like(result)

    def compute(i):
        slot = lax.rem(i, per_dev)
        load(slot).wait()
        for n, value in enumerate(walker_values(matrix, state.at[slot])):
            result[...] = jnp.where(jnp.logical_and(sub == i, lane == n), value, result[...])

        @pl.when(i < per_dev)
        def _():
            load(slot).start()

    each(0, 2 * per_dev, compute)

    def tell(n):
        target, where = readers[n]
        return remote(result, table.at[where], t_send.at[n], t_sem.at[where], target)

    for n in range(len(readers)):
        tell(n).start()

    @pl.when(hub)
    def _():
        for t in range(PARTS):
            select(t)

    table[place] = result[...]

    for t in range(PARTS):
        for s in range(per_dev):
            slot_y(s, t).wait_recv()
            slot_relay(s, t).start()

    @pl.when(hub)
    def _():
        def ended(k):
            own_to_mate(k).wait_send()
            away_to_mate(k).wait_send()
        each(0, chunks, ended)

    @pl.when(jnp.logical_not(hub))
    def _():
        each(0, chunks, lambda k: own_across(k).wait_send())

    @pl.when(row < last)
    def _():
        each(0, chunks, lambda k: send_up(k).wait_send())

    @pl.when(row > 0)
    def _():
        each(0, chunks, lambda k: send_down(k).wait_send())

    for w, t in pieces:
        walker_across(w, t).wait_send()
        walker_z(w, t).wait_send()
        walker_y(w, t).wait_send()
        walker_mate(w, t).wait_send()
        walker_relay(w, t).wait_send()
    for n in range(len(readers)):
        tell(n).wait_send()

    for j in range(1, n_vec):
        v = lax.rem(vec + j, n_vec)
        remote(result, table.at[0], t_send.at[0], t_sem.at[col * n_vec + v], mate).wait_recv()
    for j in range(n_vec):
        remote(result, table.at[0], t_send.at[0], t_sem.at[(1 - col) * n_vec + j], mate).wait_recv()
    for j in range(2 * n_vec):
        remote(result, table.at[0], t_send.at[0], t_sem.at[2 * n_vec + j], mate).wait_recv()

    for t in range(PARTS):
        for s in range(per_dev):
            slot_y(s, t).wait_send()
            slot_mate(s, t).wait()
            slot_relay(s, t).wait()
            slot_self(s, t).wait()


def step_all(n_walk, n_vec, flags, slots, chol, walkers):
    per_dev, height, width = walkers.shape
    electrons, orbitals = chol.shape[2:]
    chunks = CHUNKS if electrons % (CHUNKS * 16) == 0 else 1
    depth = electrons // chunks
    big = pltpu.VMEM((chunks, depth, orbitals), chol.dtype)
    dma = pltpu.SemaphoreType.DMA
    any_spec = pl.BlockSpec(memory_space=pl.ANY)
    smem = pl.BlockSpec(memory_space=pltpu.SMEM)
    same = jax.ShapeDtypeStruct(walkers.shape, walkers.dtype)
    piece_sem = dma((per_dev, PARTS))
    return pl.pallas_call(
        functools.partial(step_kernel, n_walk, n_vec),
        out_shape=(jax.ShapeDtypeStruct((4 * n_vec, 8, 128), jnp.float32), same, same),
        in_specs=[smem, smem, any_spec, any_spec],
        out_specs=(pl.BlockSpec(memory_space=pltpu.VMEM), any_spec, any_spec),
        scratch_shapes=[
            big, big, big, big, big,
            pltpu.VMEM((3 * per_dev, height // n_vec // PARTS, width), walkers.dtype),
            pltpu.VMEM((3 * per_dev, height // n_vec // PARTS, width), walkers.dtype),
            pltpu.VMEM((per_dev, height // n_vec, width), walkers.dtype),
            pltpu.VMEM((electrons, orbitals), chol.dtype),
            pltpu.VMEM((per_dev, height, width), walkers.dtype),
            pltpu.VMEM((8, 128), jnp.float32),
        ] + [dma((chunks,))] * 9 + [piece_sem] * 4 + [dma((per_dev, 2 * PARTS))]
        + [piece_sem] * 13 + [dma((per_dev,)), dma((4 * n_vec - 1,)), dma((4 * n_vec,))],
        compiler_params=pltpu.CompilerParams(
            collective_id=0, has_side_effects=True, vmem_limit_bytes=60 * 1024 * 1024),
        name="step_all",
    )(flags, slots, chol, walkers)


def shards(n_walk, n_vec, walkers, chol, owners, branch_src):
    per_dev = walkers.shape[0]
    walk, vec = lax.axis_index("walk"), lax.axis_index("vec")
    row, col, low = walk // 2, walk % 2, vec % 2
    swap = [(i, i + 1 - 2 * (i % 2)) for i in range(n_vec)]
    mate_roots = lax.ppermute(owners[0], "vec", swap)
    roots = jnp.where(low == col, owners[0], mate_roots)
    root = jnp.take(roots, low)
    flags = jnp.stack([root // 2 == row, root // 2 <= row, root % 2 == col]).astype(jnp.int32)
    total = per_dev * n_walk
    relative = ((branch_src - (walk - 1) * per_dev + total) % total).astype(jnp.int32)
    table, _, branched = step_all(n_walk, n_vec, flags, relative, chol, walkers)
    table = table[:, :2 * per_dev, :4].reshape(2, 2, n_vec // 2, 2, 2, per_dev, 4)
    even, odd = table[:, 0], table[:, 1]
    first = jnp.stack([even[:, :, :, 0], odd[:, :, :, 1]], axis=2)
    second = jnp.stack([even[:, :, :, 1], odd[:, :, :, 0]], axis=2)
    both = jnp.stack([first, second], axis=1)
    both = jnp.transpose(both, (0, 1, 5, 2, 3, 4, 6)).reshape(4 * per_dev, n_vec, 2, 4)
    side = relative // per_dev
    block = jnp.where(side == 1, col, jnp.where(side == 2 * (1 - col), 1 - col, 3 - col))
    chosen = jnp.take(both, block * per_dev + relative % per_dev, axis=0)
    bias = lax.dynamic_slice_in_dim(chosen, vec, 1, axis=1)[:, 0, :, :2]
    energy = -0.5 * jnp.sum(chosen[..., 2:], axis=(1, 2))
    return (branched, bias, energy)


def solution(mesh):
    n_walk, n_vec = mesh.shape["walk"], mesh.shape["vec"]
    return jax.shard_map(
        functools.partial(shards, n_walk, n_vec),
        mesh=mesh,
        in_specs=(P("walk", None, None), P("vec", "walk", None, None), P("vec", None), P("walk")),
        out_specs=(P("walk", None, None), P("walk", "vec", None), P("walk", None)),
        check_vma=False,
    )
```

time: 323 us -> 233 us (0.72)
  Pallas kernels: 269 us -> 219 us
  blocking collectives: 38.4 us -> 0 us
    pallas_call x2 -> x1, Pallas kernels: 269 us -> 219 us  [step_all(): pl.pallas_call(functools.partial(step_kernel, n_walk, n_vec), out_shape=(...]
    all_gather x1 -> x0, blocking collectives: 38.4 us -> none  [shards(): table = lax.all_gather(values, ('walk', 'vec'))]
    unnamed x3 -> x1, local copies, waits for them, and re-layouts: 8.35 us -> 6.69 us
  transfers between devices with their start and end apart: 1 -> 1, of which waited for: 0 -> 0; matrix products, arithmetic and copies ran while one was open for 0% -> 1% of each run, Pallas kernels for 0% -> 0%
where the time goes in v2:
time: 233 us
  Pallas kernels  219 us (94%)
  local copies, waits for them, and re-layouts  9.32 us (4%)
  other arithmetic  3.22 us (1%)
    pallas_call x1, Pallas kernels, step_all(): pl.pallas_call(functools.partial(step_kernel, n_walk, n_vec), out_shape=(...  219 us
    unnamed x1, local copies, waits for them, and re-layouts  6.69 us
  transfers between devices with their start and end apart: 1, of which 0 were waited for; matrix products, arithmetic and copies ran while one was open for 1% of the time, Pallas kernels for 0%

profile of v2, /device:TPU:0, one launch (start us, length us, event | category | flops | bytes accessed | tf_op | source)
XLA Modules:
  0.0 233.1 jit_solution(17583627775182381658)
XLA Ops:
  0.6 0.6 collective-permute-start
  1.2 1.2 compare_and_fusion
  2.4 0.0 collective-permute-done
  2.4 0.7 broadcast_select_fusion.1
  3.1 0.6 dynamic-slice.2
  4.3 0.6 add_convert_fusion.flags
  4.9 218.7 %step_all.1 = (f32[16,8,128]{2,1,0:T(8,128)}, bf16[2,2432,768]{2,1,0:T(8,128)(2,1)}, bf16[2,2432,768]{2,1,0:T(8,128)(2,1)}) custom-call(s32[3]{0:T(128)} %add_convert_fusion.flags, s32[2]{0:T(128)} %get-tuple-element.20.slots, bf16[1,1,384,4096]{3,2,1,0:T(8,128)(2,1)} %chol.1, bf16[2,2432,768]{2,1,0:T(8,128)(2,1)} %walkers.1), custom_call_target="tpu_custom_call" | custom-call | tf_op jit(solution)/shard_map/step_all/pallas_call | solution.py:403
  223.6 0.8 slice.27
  224.6 0.6 gather_fusion
  225.1 0.1 broadcast_select_fusion
  225.2 0.1 slice_reduce_fusion
  225.3 0.6 constant_dynamic-slice_fusion
  225.9 0.6 broadcast_multiply_fusion
  226.5 6.7 %copy.22 = bf16[2,2432,768]{2,1,0:T(8,128)(2,1)} copy(bf16[2,2432,768]{2,1,0:T(8,128)(2,1)} %get-tuple-element.32) | data formatting | bytes 14942208
  (8 shorter events, 0.1 us)
Async XLA Ops:
  0.6 1.8 collective-permute-start

commit v3 on v2

--- a/solution.py
+++ b/solution.py
@@ -10,7 +10,11 @@
 MESH = pl.DeviceIdType.MESH
 CHUNKS = 24
 PARTS = 2
-EARLY = (5, 9, 12, 15)
+SKEW = 3
+AHEAD = 3
+QUEUE = (12, 15, 18, 21)
+LEAF = ((5, 9, 12, 15), (9, 13, 16, 19), (17, 24), (24, 100))
+HUB = ((18, 22, 26, 30), (22, 26, 30, 100), (100, 200), (200, 200))
 
 
 def flip(index):
@@ -177,16 +181,24 @@
     def _():
         def start(k):
             own_to_home(k).start()
-            own_to_mate(k).start()
+
+            @pl.when(k < AHEAD)
+            def _():
+                own_to_mate(k).start()
+
         for w, t in pieces:
             walker_across(w, t).start()
         each(0, chunks, start)
 
     @pl.when(jnp.logical_not(hub))
     def _():
-        each(0, chunks, lambda k: own_across(k).start())
-        for w, t in pieces:
+        at = 0
+        for n, (w, t) in enumerate(pieces):
+            cut = min(QUEUE[min(n, len(QUEUE) - 1)], chunks)
+            each(at, cut, lambda k: own_across(k).start())
             walker_across(w, t).start()
+            at = cut
+        each(at, chunks, lambda k: own_across(k).start())
 
     for w in range(per_dev):
         pltpu.make_async_copy(walkers.at[w], state.at[w], load_sem.at[w]).start()
@@ -203,6 +215,11 @@
             def _():
                 own_across(i).wait_recv()
                 away_to_mate(i).start()
+
+                @pl.when(i + AHEAD < chunks)
+                def _():
+                    own_to_mate(i + AHEAD).start()
+
                 own_to_home(i).wait()
 
             @pl.when(jnp.logical_not(hub))
@@ -212,8 +229,8 @@
 
             own[i] = jnp.where(from_home, home[i], away[i])
 
-        ku = i - row
-        kd = i - (last - row)
+        ku = i - SKEW * row
+        kd = i - SKEW * (last - row)
 
         @pl.when(jnp.logical_and(ku >= 0, ku < chunks))
         def _():
@@ -252,32 +269,11 @@
         walker_mate(w, t).start()
         near_cand(w, t).start()
 
-    total = chunks + last
-    at = 0
-    for n, (w, t) in enumerate(pieces):
-        cut = min(EARLY[min(n, len(EARLY) - 1)], total)
-        each(at, cut, step)
-        at = cut
-
-        @pl.when(jnp.logical_not(hub))
-        def _():
-            arrive(w, t)
-    each(at, total, step)
-
-    @pl.when(hub)
-    def _():
-        for w, t in pieces:
-            arrive(w, t)
-
-    def finish(k):
-        matrix[pl.ds(pl.multiple_of(k * depth, depth), depth), :] = jnp.where(below_or_here, up[k], down[k])
-
-    each(0, chunks, finish)
-
     lines = 16
 
     def select(t):
         for w in range(per_dev):
+            own_cand(w, t).wait()
             near_cand(w, t).wait()
             walker_z(w, t).wait_recv()
         for s in range(per_dev):
@@ -292,17 +288,47 @@
             slot_mate(s, t).start()
             slot_self(s, t).start()
 
-    for w, t in pieces:
-        own_cand(w, t).wait()
-
-    @pl.when(jnp.logical_not(hub))
-    def _():
-        for t in range(PARTS):
-            select(t)
-
-    for w, t in pieces:
+    def pass_on(w, t):
         walker_y(w, t).wait_recv()
         walker_relay(w, t).start()
+
+    def pass_slots(t):
+        for s in range(per_dev):
+            slot_y(s, t).wait_recv()
+            slot_relay(s, t).start()
+
+    events = []
+    for times, role in ((LEAF, jnp.logical_not(hub)), (HUB, hub)):
+        for n, (w, t) in enumerate(pieces):
+            n = min(n, len(times[0]) - 1)
+            events.append((times[0][n], role, functools.partial(arrive, w, t)))
+            events.append((times[1][n], role, functools.partial(pass_on, w, t)))
+        for t in range(PARTS):
+            events.append((times[2][t], role, functools.partial(select, t)))
+            events.append((times[3][t], role, functools.partial(pass_slots, t)))
+    events.sort(key=lambda event: event[0])
+
+    def run(event):
+        @pl.when(event[1])
+        def _():
+            event[2]()
+
+    total = chunks + SKEW * last
+    at = 0
+    for event in events:
+        if event[0] < 200:
+            cut = min(event[0], total)
+            if cut > at:
+                each(at, cut, step)
+                at = cut
+            run(event)
+    each(at, total, step)
+
+    def finish(k):
+        matrix[pl.ds(pl.multiple_of(k * depth, depth), depth), :] = jnp.where(below_or_here, up[k], down[k])
+
+    each(0, chunks, finish)
+
     for w, t in pieces:
         walker_mate(w, t).wait_recv()
         walker_relay(w, t).wait_recv()
@@ -333,17 +359,11 @@
     for n in range(len(readers)):
         tell(n).start()
 
-    @pl.when(hub)
-    def _():
-        for t in range(PARTS):
-            select(t)
+    for event in events:
+        if event[0] >= 200:
+            run(event)
 
     table[place] = result[...]
-
-    for t in range(PARTS):
-        for s in range(per_dev):
-            slot_y(s, t).wait_recv()
-            slot_relay(s, t).start()
 
     @pl.when(hub)
     def _():

time: 233 us -> 181 us (0.78)
  the two profiles are of different devices: /device:TPU:0 before, /device:TPU:25 now
where the time goes in v3:
time: 181 us; the launch traced here: 180 us
  Pallas kernels  166 us (92%)
  local copies, waits for them, and re-layouts  9.32 us (5%)
  other arithmetic  3.22 us (2%)
    pallas_call x1, Pallas kernels, step_all(): pl.pallas_call(functools.partial(step_kernel, n_walk, n_vec), out_shape=(...  166 us
    unnamed x1, local copies, waits for them, and re-layouts  6.69 us
  transfers between devices with their start and end apart: 1, of which 0 were waited for; matrix products, arithmetic and copies ran while one was open for 1% of the time, Pallas kernels for 0%

profile of v3, /device:TPU:25, one launch (start us, length us, event | category | flops | bytes accessed | tf_op | source)
XLA Modules:
  0.0 180.4 jit_solution(14344939683840554334)
XLA Ops:
  0.6 0.7 collective-permute-start
  1.4 1.2 compare_and_fusion
  2.6 0.0 collective-permute-done
  2.6 0.7 broadcast_select_fusion.1
  3.2 0.6 dynamic-slice.2
  4.5 0.6 add_convert_fusion.flags
  5.1 165.8 %step_all.1 = (f32[16,8,128]{2,1,0:T(8,128)}, bf16[2,2432,768]{2,1,0:T(8,128)(2,1)}, bf16[2,2432,768]{2,1,0:T(8,128)(2,1)}) custom-call(s32[3]{0:T(128)} %add_convert_fusion.flags, s32[2]{0:T(128)} %get-tuple-element.20.slots, bf16[1,1,384,4096]{3,2,1,0:T(8,128)(2,1)} %chol.1, bf16[2,2432,768]{2,1,0:T(8,128)(2,1)} %walkers.1), custom_call_target="tpu_custom_call" | custom-call | tf_op jit(solution)/shard_map/step_all/pallas_call | solution.py:423
  170.9 0.8 slice.27
  171.9 0.6 gather_fusion
  172.4 0.1 broadcast_select_fusion
  172.5 0.1 slice_reduce_fusion
  172.6 0.6 constant_dynamic-slice_fusion
  173.2 0.6 broadcast_multiply_fusion
  173.7 6.7 %copy.22 = bf16[2,2432,768]{2,1,0:T(8,128)(2,1)} copy(bf16[2,2432,768]{2,1,0:T(8,128)(2,1)} %get-tuple-element.32) | data formatting | bytes 14942208
  (8 shorter events, 0.1 us)
Async XLA Ops:
  0.6 1.9 %collective-permute-start = (s32[2]{0:T(128)}, s32[2]{0:T(128)S(1)}, u32[]{:S(2)}, u32[]{:S(2)}) collective-permute-start(s32[2]{0:T(128)} %bitcast.35), channel_id=1, source_target_pairs={{0,1},{1,0},{2,3},{3,2},{4,5},{5,4},{6,7},{7,6},{8,9},{9,8},{10,11... | collective-permute-start | bytes 32 | tf_op jit(solution)/shard_map/ppermute | solution.py:449

commit v4 on v3

--- a/solution.py
+++ b/solution.py
@@ -10,11 +10,11 @@
 MESH = pl.DeviceIdType.MESH
 CHUNKS = 24
 PARTS = 2
-SKEW = 3
+SKEW = 2
 AHEAD = 3
-QUEUE = (12, 15, 18, 21)
-LEAF = ((5, 9, 12, 15), (9, 13, 16, 19), (17, 24), (24, 100))
-HUB = ((18, 22, 26, 30), (22, 26, 30, 100), (100, 200), (200, 200))
+QUEUE = (12, 14, 16, 18)
+LEAF = ((3, 6, 9, 12), (6, 9, 12, 15), (12, 17), (17, 22))
+HUB = ((16, 18, 20, 22), (19, 21, 23, 25), (24, 29), (29, 200))
 
 
 def flip(index):

time: 181 us -> 171 us (0.945)
  the two profiles are of different devices: /device:TPU:25 before, /device:TPU:0 now
where the time goes in v4:
time: 171 us; the launch traced here: 170 us
  Pallas kernels  156 us (91%)
  local copies, waits for them, and re-layouts  9.32 us (5%)
  other arithmetic  3.22 us (2%)
    pallas_call x1, Pallas kernels, step_all(): pl.pallas_call(functools.partial(step_kernel, n_walk, n_vec), out_shape=(...  156 us
    unnamed x1, local copies, waits for them, and re-layouts  6.69 us
  transfers between devices with their start and end apart: 1, of which 0 were waited for; matrix products, arithmetic and copies ran while one was open for 1% of the time, Pallas kernels for 0%

profile of v4, /device:TPU:0, one launch (start us, length us, event | category | flops | bytes accessed | tf_op | source)
XLA Modules:
  0.0 170.5 jit_solution(2825253945605552678)
XLA Ops:
  0.6 0.6 collective-permute-start
  1.2 1.2 compare_and_fusion
  2.4 0.0 collective-permute-done
  2.4 0.7 broadcast_select_fusion.1
  3.1 0.6 dynamic-slice.2
  4.3 0.6 add_convert_fusion.flags
  4.9 156.0 %step_all.1 = (f32[16,8,128]{2,1,0:T(8,128)}, bf16[2,2432,768]{2,1,0:T(8,128)(2,1)}, bf16[2,2432,768]{2,1,0:T(8,128)(2,1)}) custom-call(s32[3]{0:T(128)} %add_convert_fusion.flags, s32[2]{0:T(128)} %get-tuple-element.20.slots, bf16[1,1,384,4096]{3,2,1,0:T(8,128)(2,1)} %chol.1, bf16[2,2432,768]{2,1,0:T(8,128)(2,1)} %walkers.1), custom_call_target="tpu_custom_call" | custom-call | tf_op jit(solution)/shard_map/step_all/pallas_call | solution.py:423
  160.9 0.8 slice.27
  161.9 0.6 gather_fusion
  162.4 0.1 broadcast_select_fusion
  162.5 0.1 slice_reduce_fusion
  162.6 0.6 constant_dynamic-slice_fusion
  163.2 0.6 broadcast_multiply_fusion
  163.8 6.7 %copy.22 = bf16[2,2432,768]{2,1,0:T(8,128)(2,1)} copy(bf16[2,2432,768]{2,1,0:T(8,128)(2,1)} %get-tuple-element.32) | data formatting | bytes 14942208
  (8 shorter events, 0.1 us)
Async XLA Ops:
  0.6 1.8 %collective-permute-start = (s32[2]{0:T(128)}, s32[2]{0:T(128)S(1)}, u32[]{:S(2)}, u32[]{:S(2)}) collective-permute-start(s32[2]{0:T(128)} %bitcast.35), channel_id=1, source_target_pairs={{0,1},{1,0},{2,3},{3,2},{4,5},{5,4},{6,7},{7,6},{8,9},{9,8},{10,11... | collective-permute-start | bytes 32 | tf_op jit(solution)/shard_map/ppermute | solution.py:449
